TPU v7x, 32 devices: a whole 2x2x4 slice. The times are simulated.
32 devices in a mesh: dp: 16 (over z, y, core), mp: 2 (over x).
Axes of the slice: x: 2, y: 2, z: 4, core: 2. Of those that a mesh axis runs over, the one named last changes fastest.
Arguments:
- hidden_in: bfloat16 [8192, 4096], P('dp'), may hold values from -1.5 to 1.5
- w_query: bfloat16 [4096, 4096], P('dp', 'mp'), may hold values from -1 to 1
- w_key: bfloat16 [4096, 1024], P('dp', 'mp'), may hold values from -24 to 24
- w_value: bfloat16 [4096, 1024], P('dp', 'mp'), may hold values from -1 to 1
- w_out: bfloat16 [4096, 4096], P('dp', 'mp'), may hold values from -1 to 1
- value_weight: float32 [4096], P('mp'), may hold values from -0.09375 to 0.09375
- rewards: float32 [8192], P('dp'), may hold values from -0.6 to 0.6
- old_values: float32 [8192], P('dp'), may hold values from -6 to 6
- lengths: int32 [64], replicated, may hold values from 1 to 2048, 8192 in all
- terminal: int32 [64], replicated, may hold values 0 or 1
Outputs:
- value: float32 [8192], P('dp')
- advantage: float32 [8192], P('dp')
- value_loss: float32 [], replicated
All inputs are finite; a program needn't handle non-finite values.
Results may differ from a plain program's by a relative error of at most 0.012.
The roundings to bfloat16 on the way count: a program that leaves them out, or rounds other values in their place, can miss the bound.
Values may be sent and summed in bfloat16 or wider, within the bound.
No kernel may reach another device: no remote copies, remote signals or barrier semaphores. Data moves between devices by JAX's collectives and lax.ppermute only.
A program may use at most 128 MiB of HBM per device.

v0:
```python
import jax
import jax.numpy as jnp
from jax import lax
from jax.sharding import PartitionSpec as P

HEAD = 128
discount = 0.999
trace_decay = 0.997
clip_range = 0.2
epsilon = 1e-05
rope_base = 500000.0


def from_behind(array, axis, by):
    size = lax.axis_size(axis)
    pairs = [(i, i + by) for i in range(size) if 0 <= i + by < size]
    return lax.ppermute(array, axis, pairs)


def carried_in(part, axis, combine, identity):
    count = lax.axis_size(axis)
    place = lax.axis_index(axis)
    ahead = count - 1 - place
    gathered = jax.tree.map(lambda a: lax.all_gather(a, axis), part)
    state = jax.tree.map(lambda a, e: jnp.zeros_like(a) + jnp.asarray(e, a.dtype), part, identity)

    def one(hop, state):
        source = count - 1 - hop
        return combine(
            state, jax.tree.map(lambda a: lax.dynamic_index_in_dim(a, source, 0, False), gathered)
        )

    return lax.fori_loop(0, ahead, one, state)


def rotate(states, positions):
    half = HEAD // 2
    freq = rope_base ** (-jnp.arange(half, dtype=jnp.float32) * 2.0 / HEAD)
    angles = positions[:, None] * freq[None, :]
    cosine = jnp.cos(angles)[:, None, :]
    sine = jnp.sin(angles)[:, None, :]
    first = states[..., :half]
    second = states[..., half:]
    return jnp.concatenate([first * cosine - second * sine, second * cosine + first * sine], -1)


def body(
    hidden_in, w_query, w_key, w_value, w_out, value_weight, rewards, old_values, lengths, terminal
):
    rows = hidden_in.shape[0]
    width = hidden_in.shape[1]
    states = hidden_in.astype(jnp.float32)
    normed = (states * lax.rsqrt(jnp.mean(states * states, 1, keepdims=True) + epsilon)).astype(
        jnp.bfloat16
    )
    pieces = (
        lax.all_gather(w_query, "dp", axis=0, tiled=True),
        lax.all_gather(w_key, "dp", axis=0, tiled=True),
        lax.all_gather(w_value, "dp", axis=0, tiled=True),
        lax.all_gather(w_out, "dp", axis=0, tiled=True),
    )
    add_pieces = pieces[:3]
    summed = tuple(
        (jnp.dot(normed, piece, preferred_element_type=jnp.float32) for piece in add_pieces)
    )
    stored = pieces[3]
    query_sum, key_sum, value_sum, whole_out = summed + (stored,)
    position_ids = lax.axis_index("dp") * rows + jnp.arange(rows, dtype=jnp.int32)
    positions = position_ids.astype(jnp.float32)
    local_heads = w_query.shape[1] // HEAD
    local_kv = w_key.shape[1] // HEAD
    group = local_heads // local_kv
    query = rotate(query_sum.reshape(rows, local_heads, HEAD), positions).astype(jnp.bfloat16)
    key = rotate(key_sum.reshape(rows, local_kv, HEAD), positions).astype(jnp.bfloat16)
    values_proj = value_sum.astype(jnp.bfloat16).reshape(rows, local_kv, HEAD)
    ends = jnp.cumsum(lengths)
    matches = ends[None, :] - 1 == position_ids[:, None]
    finished = jnp.any(matches, 1).astype(jnp.float32)
    stopped = jnp.sum(jnp.where(matches, terminal[None, :], 0), 1).astype(jnp.float32)
    episode = jnp.sum((ends[None, :] <= position_ids[:, None]).astype(jnp.int32), 1)
    order = jnp.arange(rows, dtype=jnp.int32)
    same_episode = episode[None, :] == episode[:, None]
    allowed = (order[None, :] <= order[:, None]) & same_episode
    scores = jnp.einsum(
        "tkgd,skd->kgts",
        query.reshape(rows, local_kv, group, HEAD),
        key,
        preferred_element_type=jnp.float32,
    ) * (1.0 / HEAD**0.5)
    masked = jnp.where(allowed[None, None], scores, -1e30)
    largest = jnp.max(masked, -1, keepdims=True)
    expon = jnp.where(allowed[None, None], jnp.exp(masked - largest), 0.0)
    probs = (expon / jnp.sum(expon, -1, keepdims=True)).astype(jnp.bfloat16)
    output = jnp.einsum("kgts,skd->tkgd", probs, values_proj, preferred_element_type=jnp.float32)
    attended = output.astype(jnp.bfloat16).reshape(rows, local_heads * HEAD)
    all_heads = lax.all_gather(attended, "mp", axis=1, tiled=True)
    projected = jnp.dot(all_heads, whole_out, preferred_element_type=jnp.float32)
    feature_count = w_out.shape[1]
    own_states = lax.dynamic_slice_in_dim(
        states, lax.axis_index("mp") * feature_count, feature_count, 1
    )
    residual = own_states + projected
    square_sum, head_sum = lax.psum(
        (jnp.sum(residual * residual, 1), jnp.sum(residual * value_weight[None, :], 1)), "mp"
    )
    value = head_sum * lax.rsqrt(square_sum / width + epsilon)
    following = from_behind(old_values[:1], "dp", -1)
    next_old = jnp.concatenate([old_values[1:], following])
    booted = jnp.where(finished > 0, (1.0 - stopped) * old_values, next_old)
    delta = rewards + discount * booted - old_values
    keep_rate = discount * trace_decay
    spacing = (order[None, :] - order[:, None]).astype(jnp.float32)
    forward_mask = (spacing >= 0.0) & same_episode
    decay_matrix = jnp.where(
        forward_mask, jnp.power(jnp.float32(keep_rate), jnp.maximum(spacing, 0.0)), 0.0
    )
    local_part = jnp.dot(decay_matrix, delta, precision=lax.Precision.HIGHEST)
    remaining = (rows - order).astype(jnp.float32)
    reach = jnp.where(episode == episode[-1], jnp.power(jnp.float32(keep_rate), remaining), 0.0) * (
        1.0 - finished[-1]
    )

    def compose(earlier, later_map):
        return (later_map[0] + later_map[1] * earlier[0], later_map[1] * earlier[1])

    prefix = carried_in(
        (local_part[:1], reach[:1]),
        "dp",
        compose,
        (jnp.zeros((1,), jnp.float32), jnp.ones((1,), jnp.float32)),
    )
    incoming = prefix[0][0]
    advantage = local_part + reach * incoming
    returns = advantage + old_values
    clipped = old_values + jnp.clip(value - old_values, -clip_range, clip_range)
    terms = jnp.maximum((value - returns) ** 2, (clipped - returns) ** 2)
    total_loss = lax.psum(jnp.sum(terms), "dp")
    value_loss = 0.5 * total_loss / (rows * lax.axis_size("dp"))
    return (value, advantage, value_loss)


def solution(mesh):
    return jax.shard_map(
        body,
        mesh=mesh,
        in_specs=(
            P("dp", None),
            P("dp", "mp"),
            P("dp", "mp"),
            P("dp", "mp"),
            P("dp", "mp"),
            P("mp"),
            P("dp"),
            P("dp"),
            P(),
            P(),
        ),
        out_specs=(P("dp"), P("dp"), P()),
        check_vma=False,
    )
```

profile of v0, /device:TPU:0, one launch (start us, length us, event | category | flops | bytes accessed | tf_op | source)
XLA Modules:
  0.0 487.3 jit_solution(12846572343256018310)
XLA Ops:
  7.2 0.7 all-gather.10.cloned.1.call-update
  7.9 0.7 all-gather.8.cloned.1.call-update
  8.7 0.7 all-gather.12.cloned.1.call-update
  9.4 0.5 all-gather.16.cloned.1.call-update
  10.0 0.0 all-gather.14.cloned.1.call-start
  10.0 0.7 copy.25
  10.8 0.1 reduce-window.7
  10.9 0.1 reduce
  11.0 0.8 fusion.22
  11.8 3.1 multiply_reduce_fusion
  14.9 0.2 compare_and_fusion.1
  15.1 1.0 multiply_cosine_fusion
  16.1 47.2 %all-gather.10.cloned.1.call-done = bf16[4096,512]{1,0:T(8,128)(2,1)} async-done(((bf16[256,512]{1,0:T(8,128)(2,1)}), bf16[4096,512]{1,0:T(8,128)(2,1)}) %all-gather.10.cloned.1.call-update) | async-done | bytes 4194320 | tf_op jit(solution)/shard_map/all_gather | solution.py:58
  63.3 5.9 %fusion.32 = f32[512,512]{0,1:T(8,128)S(1)} fusion(bf16[4096,512]{1,0:T(8,128)(2,1)} %all-gather.10.cloned.1.call-done, f32[512]{0:T(512)S(1)} %add_rsqrt_fusion, bf16[512,4096]{1,0:T(8,128)(2,1)} %param.12), kind=kOutput, calls=%fused_computation.70 | convolution fusion | flops 2153775104 | bytes 9439232 | tf_op jit(solution)/shard_map/dot_general | solution.py:64
  69.2 0.1 fusion.33
  69.3 0.3 copy.34
  69.6 0.3 copy.35
  69.9 1.1 subtract_convert_fusion.1
  71.0 43.3 %all-gather.8.cloned.1.call-done = bf16[4096,512]{1,0:T(8,128)(2,1)} async-done(((bf16[256,512]{1,0:T(8,128)(2,1)}), bf16[4096,512]{1,0:T(8,128)(2,1)}) %all-gather.8.cloned.1.call-update) | async-done | bytes 4194320 | tf_op jit(solution)/shard_map/all_gather | solution.py:59
  114.4 5.9 %convolution_convert_fusion = bf16[512,512]{0,1:T(8,128)(2,1)S(1)} fusion(bf16[4096,512]{1,0:T(8,128)(2,1)} %all-gather.8.cloned.1.call-done, f32[512]{0:T(512)S(1)} %add_rsqrt_fusion, bf16[512,4096]{1,0:T(8,128)(2,1)} %param.12), kind=kOutput, calls=%fused_computation.26 | convolution fusion | flops 2154037248 | bytes 8914944 | tf_op jit(solution)/shard_map/dot_general | solution.py:64
  120.3 121.2 %all-gather.12.cloned.1.call-done = bf16[4096,2048]{1,0:T(8,128)(2,1)} async-done(((bf16[256,2048]{1,0:T(8,128)(2,1)}), bf16[4096,2048]{1,0:T(8,128)(2,1)}) %all-gather.12.cloned.1.call-update) | async-done | bytes 16777232 | tf_op jit(solution)/shard_map/all_gather | solution.py:57
  241.5 13.2 %convolution_bitcast_fusion = f32[64,8,16,128]{3,1,2,0:T(8,128)S(1)} fusion(bf16[4096,2048]{1,0:T(8,128)(2,1)} %all-gather.12.cloned.1.call-done, f32[512]{0:T(512)S(1)} %add_rsqrt_fusion, bf16[512,4096]{1,0:T(8,128)(2,1)} %param.12), kind=kOutput, calls=%fused_computation.18 | convolution fusion | flops 8596226048 | bytes 25167872 | tf_op jit(solution)/shard_map/dot_general | solution.py:64
  254.8 0.9 copy.36
  255.7 1.8 subtract_convert_fusion
  257.5 0.5 copy.29
  258.1 0.5 copy.28
  258.6 8.1 %fusion.6 = f32[4,512,512,4]{2,1,3,0:T(8,128)} fusion(bf16[512,4,4,64]{3,0,2,1:T(8,128)(2,1)S(1)} %bitcast.53, bf16[512,4,4,64]{3,0,2,1:T(8,128)(2,1)S(1)} %bitcast.54, bf16[512,4,64]{2,0,1:T(8,128)(2,1)S(1)} %copy-done, bf16[512,4,64]{2,0,1:T(8,128)(2,1)S(1)} %get-tuple-element.113), kind=kOutput, calls=%fused_computation.19 | convolution fusion | flops 1078984704 | bytes 19398656 | tf_op jit(solution)/shard_map/tkgd,skd->kgts/dot_general | solution.py:84
  266.8 17.9 %fusion.34 = (f32[4,4,512]{2,1,0:T(4,128)S(1)}, f32[4,4,512,512]{2,3,1,0:T(8,128)}) fusion(f32[4,512,512,4]{2,1,3,0:T(8,128)} %fusion.6, pred[512,512]{0,1:T(8,128)(4,1)S(1)} %compare_and_fusion.1), kind=kOutput, calls=%fused_computation.72 | output fusion | flops 29360640 | bytes 33849344 | tf_op jit(solution)/shard_map/sub | solution.py:92
  284.7 8.6 %fusion.10 = bf16[4,128,4,512]{3,1,2,0:T(8,128)(2,1)} fusion(bf16[512,4,128,1]{0,2,3,1:T(8,128)(2,1)S(1)} %bitcast.63, f32[4,4,512,512]{2,3,1,0:T(8,128)} %get-tuple-element.120, f32[4,4,512]{2,1,0:T(4,128)S(1)} %get-tuple-element.119), kind=kOutput, calls=%fused_computation.23 | convolution fusion | flops 1083179008 | bytes 19431424 | tf_op jit(solution)/shard_map/kgts,skd->tkgd/dot_general | solution.py:94
  293.4 0.5 slice.35
  293.9 1.3 collective-permute-start
  295.2 6.5 %convert_element_type.45 = f32[512,4096]{1,0:T(8,128)} convert(bf16[512,4096]{1,0:T(8,128)(2,1)} %param.12) | non-fusion elementwise | flops 2097152 | bytes 12582912 | tf_op jit(solution)/shard_map/convert_element_type | solution.py:52
  301.7 0.6 slice.36
  302.4 0.1 slice.34
  302.4 0.1 compare_reduce_fusion
  302.5 0.6 slice.37
  303.8 0.6 dynamic-slice
  304.4 0.7 select_multiply_fusion
  305.1 0.7 slice_dynamic-update-slice_fusion
  305.8 0.7 fusion.25
  306.5 1.1 fusion.11
  307.6 0.7 slice_dynamic-update-slice_fusion.1
  308.3 34.8 %all-reduce.2 = (f32[16]{0:T(128)S(1)}, f32[16]{0:T(128)S(1)}) all-reduce(f32[16]{0:T(128)S(1)} %slice_dynamic-update-slice_fusion.1, f32[16]{0:T(128)S(1)} %slice_dynamic-update-slice_fusion), channel_id=2, replica_groups=mesh['dp'=16,'mp'=2] {'dp'}, use_global_device_ids=true, to_apply=%add | all-reduce | flops 32 | bytes 256
  343.1 28.6 %while.14 = (s32[]{:T(128)}, f32[1]{0:T(128)}, s32[]{:T(128)}, f32[16,1]{0,1:T(1,128)S(1)}, f32[16,1]{0,1:T(1,128)S(1)}, /*index=5*/s32[]{:T(128)}, s32[]{:T(128)}, s32[]{:T(128)}, s32[]{:T(128)}) while((s32[]{:T(128)}, f32[1]{0:T(128)}, s32[]{:T(128)}, f32[16,1]{0,1:T(1,128)S(1)}, f32[16,1]{0,1:T(1,128)S(1)}, /*index=5*/s32[]{:T(128)}, ...), condition=%wide.region_12.13_spmd, body=%wide.region_11.12_spmd.sunk | while | flops 8 | bytes 183 | solution.py:33
  343.1 0.6 constant_dynamic-slice_fusion.3
  345.0 0.6 constant_dynamic-slice_fusion.3
  346.9 0.6 constant_dynamic-slice_fusion.3
  348.9 0.6 constant_dynamic-slice_fusion.3
  350.8 0.6 constant_dynamic-slice_fusion.3
  352.7 0.6 constant_dynamic-slice_fusion.3
  354.6 0.6 constant_dynamic-slice_fusion.3
  356.5 0.6 constant_dynamic-slice_fusion.3
  358.4 0.6 constant_dynamic-slice_fusion.3
  360.3 0.6 constant_dynamic-slice_fusion.3
  362.2 0.6 constant_dynamic-slice_fusion.3
  364.1 0.6 constant_dynamic-slice_fusion.3
  366.0 0.6 constant_dynamic-slice_fusion.3
  367.9 0.6 constant_dynamic-slice_fusion.3
  369.8 0.6 constant_dynamic-slice_fusion.3
  371.7 53.4 %all-gather.14.cloned.1.call-done = bf16[512,4096]{0,1:T(8,128)(2,1)} async-done(((bf16[512,2048]{0,1:T(8,128)(2,1)}), bf16[512,4096]{0,1:T(8,128)(2,1)}) %all-gather.14.cloned.1.call-update) | async-done | bytes 4194320 | tf_op jit(solution)/shard_map/all_gather | solution.py:96
  425.1 14.6 %multiply_reduce_fusion.1 = (f32[512]{0:T(512)S(1)}, f32[512]{0:T(512)S(1)}) fusion(f32[2048]{0:T(1024)S(1)} %copy-done.3, bf16[512,4096]{0,1:T(8,128)(2,1)} %all-gather.14.cloned.1.call-done, bf16[4096,2048]{1,0:T(8,128)(2,1)} %all-gather.16.cloned.1.call-done, f32[512,4096]{1,0:T(8,128)} %convert_element_type.45, s32[]{:T(128)S(6)} %select_n.35), kind=kOutput, calls=%fused_computation.13 | convolution fusion | flops 8595177472 | bytes 25178116 | tf_op jit(solution)/shard_map/dot_general | solution.py:97
  439.7 4.9 %all-reduce.3 = (f32[512]{0:T(512)S(1)}, f32[512]{0:T(512)S(1)}) all-reduce(f32[512]{0:T(512)S(1)} %get-tuple-element.89, f32[512]{0:T(512)S(1)} %get-tuple-element.88), channel_id=1, replica_groups=mesh['dp'=16,'mp'=2] {'mp'}, use_global_device_ids=true, to_apply=%region_6.7 | all-reduce | flops 1024 | bytes 8192 | tf_op jit(solution)/shard_map/psum | solution.py:103
  444.7 1.9 maximum_reduce_fusion
  446.5 32.5 %psum.23 = f32[]{:T(128)} all-reduce(f32[]{:T(128)} %get-tuple-element.106), channel_id=1, replica_groups=mesh['dp'=16,'mp'=2] {'dp'}, use_global_device_ids=true, to_apply=%region_14.15 | all-reduce | flops 1 | bytes 8 | tf_op jit(solution)/shard_map/psum | solution.py:137
  (25 shorter events, 0.3 us)
Async XLA Ops:
  7.2 56.1 %all-gather.10.cloned.1.call-start = ((), (), s32[]{:S(2)}) async-start(), calls=%async_computation.1 | async-start | bytes 4456448 | tf_op jit(solution)/shard_map/all_gather | solution.py:58
  7.9 106.5 %all-gather.8.cloned.1.call-start = ((), (), s32[]{:S(2)}) async-start(), calls=%async_computation | async-start | bytes 4456448 | tf_op jit(solution)/shard_map/all_gather | solution.py:59
  8.7 232.9 %all-gather.12.cloned.1.call-start = ((), (), s32[]{:S(2)}) async-start(), calls=%async_computation.2 | async-start | bytes 17825792 | tf_op jit(solution)/shard_map/all_gather | solution.py:57
  9.4 362.3 %all-gather.16.cloned.1.call-start = ((), (), s32[]{:S(2)}) async-start(), calls=%async_computation.4 | async-start | bytes 17825792 | tf_op jit(solution)/shard_map/all_gather | solution.py:60
  10.0 415.2 %all-gather.14.cloned.1.call-start = ((), (), s32[]{:S(2)}) async-start(), calls=%async_computation.3 | async-start | bytes 6291456 | tf_op jit(solution)/shard_map/all_gather | solution.py:96
  257.5 1.1 copy-start
  284.7 8.6 %copy-start.1 = (f32[512]{0:T(512)S(1)}, f32[512]{0:T(512)}, u32[]{:S(2)}) copy-start(f32[512]{0:T(512)} %param.19) | copy-start | bytes 6148
  293.9 12.0 %collective-permute-start = (f32[1]{0:T(128)}, f32[1]{0:T(128)}, u32[]{:S(2)}, u32[]{:S(2)}) collective-permute-start(f32[1]{0:T(128)} %slice.35), channel_id=1, source_target_pairs={{2,0},{4,2},{6,4},{8,6},{10,8},{12,10},{14,12},{16,14},{18,16},{20... | collective-permute-start | bytes 20 | tf_op jit(solution)/shard_map/ppermute | solution.py:17
  295.2 8.6 %copy-start.4 = (u32[32]{0:T(128)S(1)}, u32[32]{0:T(128)}, u32[]{:S(2)}) copy-start(u32[32]{0:T(128)} %constant.106) | copy-start | bytes 388
  295.2 10.7 %copy-start.2 = (f32[512]{0:T(512)S(1)}, f32[512]{0:T(512)}, u32[]{:S(2)}) copy-start(f32[512]{0:T(512)} %param.18) | copy-start | bytes 6148
  295.2 130.0 %copy-start.3 = (f32[2048]{0:T(1024)S(1)}, f32[2048]{0:T(1024)}, u32[]{:S(2)}) copy-start(f32[2048]{0:T(1024)} %param.17) | copy-start | bytes 24580
Sparse Core Ops, SparseCore 0:
  10.1 53.0 all-gather.9
  65.4 48.8 all-gather.7
  116.5 124.9 all-gather.11
  243.6 125.2 all-gather.15
  370.2 54.8 all-gather.13
where the time goes:
time: 488 us; the launch traced here: 487 us
  waiting for transfers between devices  268 us (55%)
  blocking collectives  72.2 us (15%)
  matrix products  57.5 us (12%)
  other arithmetic  36 us (7%)
  loops' own time  19.3 us (4%)
  local copies, waits for them, and re-layouts  16.7 us (3%)
  between operations  16.4 us (3%)
    all_gather x1, waiting for transfers between devices, body(): lax.all_gather(w_query, 'dp', axis=0, tiled=True)  121 us
    all_gather x1, waiting for transfers between devices, body(): all_heads = lax.all_gather(attended, 'mp', axis=1, tiled=True)  53.4 us
    all_gather x1, waiting for transfers between devices, body(): lax.all_gather(w_key, 'dp', axis=0, tiled=True)  47.2 us
    all_gather x1, waiting for transfers between devices, body(): lax.all_gather(w_value, 'dp', axis=0, tiled=True)  43.3 us
    unnamed x1, blocking collectives  34.8 us
    psum x1, blocking collectives, body(): total_loss = lax.psum(jnp.sum(terms), 'dp')  32.5 us
    dot_general x3, matrix products, body(): jnp.dot(normed, piece, preferred_element_type=jnp.float32)  25 us
    another operation x1, loops' own time, carried_in(): return lax.fori_loop(0, ahead, one, state)  19.3 us
  transfers between devices with their start and end apart: 6, of which 4 were waited for; matrix products, arithmetic and copies ran while one was open for 19% of the time, Pallas kernels for 0%

commit v1 on v0

--- a/solution.py
+++ b/solution.py
@@ -93,7 +93,7 @@
     probs = (expon / jnp.sum(expon, -1, keepdims=True)).astype(jnp.bfloat16)
     output = jnp.einsum("kgts,skd->tkgd", probs, values_proj, preferred_element_type=jnp.float32)
     attended = output.astype(jnp.bfloat16).reshape(rows, local_heads * HEAD)
-    all_heads = lax.all_gather(attended, "mp", axis=1, tiled=True)
+    all_heads = jnp.concatenate(lax.all_gather(attended, "mp"), 1)
     projected = jnp.dot(all_heads, whole_out, preferred_element_type=jnp.float32)
     feature_count = w_out.shape[1]
     own_states = lax.dynamic_slice_in_dim(

time: 488 us -> 538 us (1.10)
  waiting for transfers between devices: 268 us -> 312 us
  local copies, waits for them, and re-layouts: 16.7 us -> 26.5 us
    all_gather x1, waiting for transfers between devices: 0.02 us -> 97.9 us  [body(): lax.all_gather(w_out, 'dp', axis=0, tiled=True)]
    all_gather x1, waiting for transfers between devices: 53.4 us -> 0.02 us  [body(): all_heads = jnp.concatenate(lax.all_gather(attended, 'mp'), 1)]
    all_gather x0 -> x1, local copies, waits for them, and re-layouts: none -> 6.28 us  [body(): all_heads = jnp.concatenate(lax.all_gather(attended, 'mp'), 1)]
  transfers between devices with their start and end apart: 6 -> 6, of which waited for: 4 -> 4; matrix products, arithmetic and copies ran while one was open for 19% -> 9% of each run, Pallas kernels for 0% -> 0%
where the time goes in v1:
time: 538 us; the launch traced here: 537 us
  waiting for transfers between devices  312 us (58%)
  blocking collectives  67.2 us (12%)
  matrix products  56.5 us (11%)
  other arithmetic  36.4 us (7%)
  local copies, waits for them, and re-layouts  26.5 us (5%)
  loops' own time  20.5 us (4%)
  between operations  16.5 us (3%)
    all_gather x1, waiting for transfers between devices, body(): lax.all_gather(w_query, 'dp', axis=0, tiled=True)  120 us
    all_gather x1, waiting for transfers between devices, body(): lax.all_gather(w_out, 'dp', axis=0, tiled=True)  97.9 us
    all_gather x1, waiting for transfers between devices, body(): lax.all_gather(w_key, 'dp', axis=0, tiled=True)  47.8 us
    all_gather x1, waiting for transfers between devices, body(): lax.all_gather(w_value, 'dp', axis=0, tiled=True)  43.3 us
    unnamed x1, blocking collectives  32.1 us
    psum x1, blocking collectives, body(): total_loss = lax.psum(jnp.sum(terms), 'dp')  30.2 us
    dot_general x3, matrix products, body(): jnp.dot(normed, piece, preferred_element_type=jnp.float32)  25.6 us
    another operation x1, loops' own time, carried_in(): return lax.fori_loop(0, ahead, one, state)  20.5 us
  transfers between devices with their start and end apart: 6, of which 4 were waited for; matrix products, arithmetic and copies ran while one was open for 9% of the time, Pallas kernels for 0%

profile of v1, /device:TPU:0, one launch (start us, length us, event | category | flops | bytes accessed | tf_op | source)
XLA Modules:
  0.0 537.2 jit_solution(15235032153322067136)
XLA Ops:
  7.2 0.7 all-gather.10.cloned.1.call-update
  7.9 0.7 all-gather.8.cloned.1.call-update
  8.7 0.7 all-gather.12.cloned.1.call-update
  9.4 0.7 copy.40
  10.2 0.1 reduce-window.7
  10.3 0.1 reduce
  10.4 0.8 fusion.22
  11.2 3.1 multiply_reduce_fusion
  14.3 0.2 compare_and_fusion.1
  14.5 1.0 multiply_cosine_fusion
  15.5 47.8 %all-gather.10.cloned.1.call-done = bf16[4096,512]{1,0:T(8,128)(2,1)} async-done(((bf16[256,512]{1,0:T(8,128)(2,1)}), bf16[4096,512]{1,0:T(8,128)(2,1)}) %all-gather.10.cloned.1.call-update) | async-done | bytes 4194320 | tf_op jit(solution)/shard_map/all_gather | solution.py:58
  63.3 5.9 %fusion.32 = f32[512,512]{0,1:T(8,128)S(1)} fusion(bf16[4096,512]{1,0:T(8,128)(2,1)} %all-gather.10.cloned.1.call-done, f32[512]{0:T(512)S(1)} %add_rsqrt_fusion, bf16[512,4096]{1,0:T(8,128)(2,1)} %param.12), kind=kOutput, calls=%fused_computation.70 | convolution fusion | flops 2153775104 | bytes 9439232 | tf_op jit(solution)/shard_map/dot_general | solution.py:64
  69.2 0.1 fusion.33
  69.3 0.3 copy.51
  69.6 0.3 copy.52
  70.0 1.1 subtract_convert_fusion.1
  71.1 43.3 %all-gather.8.cloned.1.call-done = bf16[4096,512]{1,0:T(8,128)(2,1)} async-done(((bf16[256,512]{1,0:T(8,128)(2,1)}), bf16[4096,512]{1,0:T(8,128)(2,1)}) %all-gather.8.cloned.1.call-update) | async-done | bytes 4194320 | tf_op jit(solution)/shard_map/all_gather | solution.py:59
  114.4 6.7 %convolution_convert_fusion = bf16[512,512]{0,1:T(8,128)(2,1)} fusion(bf16[4096,512]{1,0:T(8,128)(2,1)} %all-gather.8.cloned.1.call-done, f32[512]{0:T(512)S(1)} %add_rsqrt_fusion, bf16[512,4096]{1,0:T(8,128)(2,1)} %param.12), kind=kOutput, calls=%fused_computation.26 | convolution fusion | flops 2154037248 | bytes 8914944 | tf_op jit(solution)/shard_map/dot_general | solution.py:64
  121.1 120.4 %all-gather.12.cloned.1.call-done = bf16[4096,2048]{1,0:T(8,128)(2,1)} async-done(((bf16[256,2048]{1,0:T(8,128)(2,1)}), bf16[4096,2048]{1,0:T(8,128)(2,1)}) %all-gather.12.cloned.1.call-update) | async-done | bytes 16777232 | tf_op jit(solution)/shard_map/all_gather | solution.py:57
  241.5 13.0 %convolution_bitcast_fusion = f32[64,8,16,128]{3,1,2,0:T(8,128)S(1)} fusion(bf16[4096,2048]{1,0:T(8,128)(2,1)} %all-gather.12.cloned.1.call-done, f32[512]{0:T(512)S(1)} %add_rsqrt_fusion, bf16[512,4096]{1,0:T(8,128)(2,1)} %param.12), kind=kOutput, calls=%fused_computation.18 | convolution fusion | flops 8596226048 | bytes 25167872 | tf_op jit(solution)/shard_map/dot_general | solution.py:64
  254.5 0.9 copy.53
  255.5 1.6 subtract_convert_fusion
  257.1 0.5 copy.44
  257.6 0.5 copy.43
  258.2 8.2 %fusion.6 = f32[4,512,512,4]{2,1,3,0:T(8,128)} fusion(bf16[512,4,4,64]{3,0,2,1:T(8,128)(2,1)S(1)} %bitcast.56, bf16[512,4,4,64]{3,0,2,1:T(8,128)(2,1)S(1)} %bitcast.57, bf16[512,4,64]{2,0,1:T(8,128)(2,1)S(1)} %copy-done, bf16[512,4,64]{2,0,1:T(8,128)(2,1)S(1)} %get-tuple-element.113), kind=kOutput, calls=%fused_computation.19 | convolution fusion | flops 1078984704 | bytes 19398656 | tf_op jit(solution)/shard_map/tkgd,skd->kgts/dot_general | solution.py:84
  266.3 17.8 %fusion.34 = (f32[4,4,512]{2,1,0:T(4,128)S(1)}, f32[4,4,512,512]{2,3,1,0:T(8,128)}) fusion(f32[4,512,512,4]{2,1,3,0:T(8,128)} %fusion.6, pred[512,512]{0,1:T(8,128)(4,1)S(1)} %compare_and_fusion.1), kind=kOutput, calls=%fused_computation.72 | output fusion | flops 29360640 | bytes 33849344 | tf_op jit(solution)/shard_map/sub | solution.py:92
  284.2 7.1 %fusion.10 = bf16[4,128,4,512]{3,1,2,0:T(8,128)(2,1)S(1)} fusion(bf16[512,4,128,1]{0,2,3,1:T(8,128)(2,1)S(1)} %bitcast.67, f32[4,4,512,512]{2,3,1,0:T(8,128)} %get-tuple-element.120, f32[4,4,512]{2,1,0:T(4,128)S(1)} %get-tuple-element.119), kind=kOutput, calls=%fused_computation.23 | convolution fusion | flops 1083179008 | bytes 19431424 | tf_op jit(solution)/shard_map/kgts,skd->tkgd/dot_general | solution.py:94
  291.2 2.5 copy.46
  293.8 0.5 all-gather.16.cloned.1.call-update
  294.4 0.5 slice.35
  294.9 1.3 collective-permute-start
  296.2 7.3 %convert_element_type.45 = f32[512,4096]{1,0:T(8,128)} convert(bf16[512,4096]{1,0:T(8,128)(2,1)} %param.12) | non-fusion elementwise | flops 2097152 | bytes 12582912 | tf_op jit(solution)/shard_map/convert_element_type | solution.py:52
  303.5 0.6 slice.36
  304.2 0.1 compare_reduce_fusion
  304.3 0.7 slice.37
  305.7 0.7 dynamic-slice
  306.3 0.7 select_multiply_fusion
  307.0 0.7 slice_dynamic-update-slice_fusion
  307.8 0.8 fusion.25
  308.5 1.1 fusion.11
  309.6 0.7 slice_dynamic-update-slice_fusion.1
  310.4 32.1 %all-reduce.2 = (f32[16]{0:T(128)S(1)}, f32[16]{0:T(128)S(1)}) all-reduce(f32[16]{0:T(128)S(1)} %slice_dynamic-update-slice_fusion.1, f32[16]{0:T(128)S(1)} %slice_dynamic-update-slice_fusion), channel_id=2, replica_groups=mesh['dp'=16,'mp'=2] {'dp'}, use_global_device_ids=true, to_apply=%add | all-reduce | flops 32 | bytes 256
  342.5 30.6 %while.14 = (s32[]{:T(128)}, f32[1]{0:T(128)}, s32[]{:T(128)}, f32[16,1]{0,1:T(1,128)S(1)}, f32[16,1]{0,1:T(1,128)S(1)}, /*index=5*/s32[]{:T(128)}, s32[]{:T(128)}, s32[]{:T(128)}, s32[]{:T(128)}) while((s32[]{:T(128)}, f32[1]{0:T(128)}, s32[]{:T(128)}, f32[16,1]{0,1:T(1,128)S(1)}, f32[16,1]{0,1:T(1,128)S(1)}, /*index=5*/s32[]{:T(128)}, ...), condition=%wide.region_12.13_spmd, body=%wide.region_11.12_spmd.sunk | while | flops 8 | bytes 183 | solution.py:33
  342.5 0.7 constant_dynamic-slice_fusion.3
  344.5 0.7 constant_dynamic-slice_fusion.3
  346.6 0.7 constant_dynamic-slice_fusion.3
  348.6 0.7 constant_dynamic-slice_fusion.3
  350.7 0.7 constant_dynamic-slice_fusion.3
  352.7 0.7 constant_dynamic-slice_fusion.3
  354.7 0.7 constant_dynamic-slice_fusion.3
  356.8 0.7 constant_dynamic-slice_fusion.3
  358.8 0.7 constant_dynamic-slice_fusion.3
  360.9 0.7 constant_dynamic-slice_fusion.3
  362.9 0.7 constant_dynamic-slice_fusion.3
  364.9 0.7 constant_dynamic-slice_fusion.3
  367.0 0.7 constant_dynamic-slice_fusion.3
  369.0 0.7 constant_dynamic-slice_fusion.3
  371.1 0.7 constant_dynamic-slice_fusion.3
  373.1 6.3 %copy.47 = bf16[2,512,2048]{1,2,0:T(8,128)(2,1)} copy(bf16[2,512,2048]{2,1,0:T(8,128)(2,1)} %all-gather.14.cloned.1.call-done) | data formatting | bytes 8388608 | tf_op jit(solution)/shard_map/all_gather | solution.py:96
  379.4 97.9 %all-gather.16.cloned.1.call-done = bf16[4096,2048]{1,0:T(8,128)(2,1)} async-done(((bf16[256,2048]{1,0:T(8,128)(2,1)}), bf16[4096,2048]{1,0:T(8,128)(2,1)}) %all-gather.16.cloned.1.call-update) | async-done | bytes 16777232 | tf_op jit(solution)/shard_map/all_gather | solution.py:60
  477.3 14.6 %multiply_reduce_fusion.1 = (f32[512]{0:T(512)S(1)}, f32[512]{0:T(512)S(1)}) fusion(f32[2048]{0:T(1024)S(1)} %copy-done.3, bf16[512,4096]{0,1:T(8,128)(2,1)} %bitcast.58, bf16[4096,2048]{1,0:T(8,128)(2,1)} %all-gather.16.cloned.1.call-done, f32[512,4096]{1,0:T(8,128)} %convert_element_type.45, s32[]{:T(128)S(6)} %select_n.35), kind=kOutput, calls=%fused_computation.13 | convolution fusion | flops 8595177472 | bytes 25178116 | tf_op jit(solution)/shard_map/dot_general | solution.py:97
  491.9 4.9 all-reduce.3
  496.9 1.9 maximum_reduce_fusion
  498.7 30.2 %psum.23 = f32[]{:T(128)} all-reduce(f32[]{:T(128)} %get-tuple-element.106), channel_id=1, replica_groups=mesh['dp'=16,'mp'=2] {'dp'}, use_global_device_ids=true, to_apply=%region_14.15 | all-reduce | flops 1 | bytes 8 | tf_op jit(solution)/shard_map/psum | solution.py:137
  (29 shorter events, 0.4 us)
Async XLA Ops:
  7.2 56.1 %all-gather.10.cloned.1.call-start = ((), (), s32[]{:S(2)}) async-start(), calls=%async_computation.1 | async-start | bytes 4456448 | tf_op jit(solution)/shard_map/all_gather | solution.py:58
  7.9 106.5 %all-gather.8.cloned.1.call-start = ((), (), s32[]{:S(2)}) async-start(), calls=%async_computation | async-start | bytes 4456448 | tf_op jit(solution)/shard_map/all_gather | solution.py:59
  8.7 232.9 %all-gather.12.cloned.1.call-start = ((), (), s32[]{:S(2)}) async-start(), calls=%async_computation.2 | async-start | bytes 17825792 | tf_op jit(solution)/shard_map/all_gather | solution.py:57
  9.4 363.7 %all-gather.14.cloned.1.call-start = ((), (), s32[]{:S(2)}) async-start(), calls=%async_computation.3 | async-start | bytes 6291456 | tf_op jit(solution)/shard_map/all_gather | solution.py:96
  257.1 1.1 copy-start
  266.3 17.8 %copy-start.4 = (bf16[512,512]{0,1:T(8,128)(2,1)S(1)}, bf16[512,512]{0,1:T(8,128)(2,1)}, u32[]{:S(2)}) copy-start(bf16[512,512]{0,1:T(8,128)(2,1)} %convolution_convert_fusion) | copy-start | bytes 1572868
  291.2 3.2 copy-start.1
  293.8 183.5 %all-gather.16.cloned.1.call-start = ((), (), s32[]{:S(2)}) async-start(), calls=%async_computation.4 | async-start | bytes 17825792 | tf_op jit(solution)/shard_map/all_gather | solution.py:60
  294.9 12.8 %collective-permute-start = (f32[1]{0:T(128)}, f32[1]{0:T(128)}, u32[]{:S(2)}, u32[]{:S(2)}) collective-permute-start(f32[1]{0:T(128)} %slice.35), channel_id=1, source_target_pairs={{2,0},{4,2},{6,4},{8,6},{10,8},{12,10},{14,12},{16,14},{18,16},{20... | collective-permute-start | bytes 20 | tf_op jit(solution)/shard_map/ppermute | solution.py:17
  296.2 9.5 %copy-start.5 = (u32[32]{0:T(128)S(1)}, u32[32]{0:T(128)}, u32[]{:S(2)}) copy-start(u32[32]{0:T(128)} %constant.106) | copy-start | bytes 388
  296.2 11.5 %copy-start.2 = (f32[512]{0:T(512)S(1)}, f32[512]{0:T(512)}, u32[]{:S(2)}) copy-start(f32[512]{0:T(512)} %param.18) | copy-start | bytes 6148
  373.1 104.2 %copy-start.3 = (f32[2048]{0:T(1024)S(1)}, f32[2048]{0:T(1024)}, u32[]{:S(2)}) copy-start(f32[2048]{0:T(1024)} %param.17) | copy-start | bytes 24580
Sparse Core Ops, SparseCore 0:
  10.1 53.0 all-gather.9
  65.4 48.8 all-gather.7
  116.5 124.9 all-gather.11
  293.9 54.8 all-gather.13
  350.8 126.4 all-gather.15
